TPU v7x, 128 devices: a whole 4x4x4 slice. The times are simulated.
128 devices in a mesh: leaf: 4 (over y), row: 4 (over z), col: 8 (over x, core).
Axes of the slice: x: 4, y: 4, z: 4, core: 2. Of those that a mesh axis runs over, the one named last changes fastest.
Arguments:
- rhs_leaf: bfloat16 [4, 12288, 256], P('leaf', 'col'), may hold values from -6 to 6
- rhs_parent: bfloat16 [16384, 256], P(('leaf', 'row', 'col')), may hold values from -6 to 6
- inv_leaf: bfloat16 [4, 12288, 12288], P('leaf', 'row', 'col'), as said below
- panel: bfloat16 [4, 6144, 12288], P('leaf', 'col', 'row'), may hold values from -0.0546875 to 0.0546875
- row_map: int32 [4, 6144], P('leaf', 'col'), may hold values from 0 to 16383, as said below
- inv_parent: bfloat16 [16384, 16384], P(('row', 'col'), 'leaf'), as said below
Outputs:
- sol_leaf: bfloat16 [4, 12288, 256], P('leaf', 'col')
- sol_parent: bfloat16 [16384, 256], P(('leaf', 'row', 'col'))
Inputs may be any that keep to these rules, and one draw needn't show every extreme that they name: Within one leaf the 6144 entries of row_map are distinct parent rows. Split the parent rows into 128 owner blocks of 16384 // 128 consecutive rows: in each aligned block of 192 consecutive entries of a leaf, at most 2 entries fall in one owner block, and exactly 2 in some. `inv_leaf`: lower triangular: zeros above the diagonal, diagonal entries between 0.5 and 2. `inv_parent`: lower triangular: zeros above the diagonal, diagonal entries between 0.5 and 2.
All inputs are finite; a program needn't handle non-finite values.
Results may differ from a plain program's by a relative error of at most 0.01.
Values may be sent and summed in bfloat16 or wider, within the bound.
A program may use at most 128 MiB of HBM per device.

v0:
```python
import jax
import jax.numpy as jnp
from jax import lax
from jax.sharding import PartitionSpec as P


def dense_updates(update, row_map, rhs_parent):
    total_rows = rhs_parent.shape[0] * lax.axis_size(("leaf", "row", "col"))
    dense = jnp.zeros((total_rows, rhs_parent.shape[1]), jnp.float32)
    dense = dense.at[row_map[0]].add(-update)
    offset = lax.axis_index(("leaf", "row", "col")) * rhs_parent.shape[0]
    own_rows = lax.dynamic_slice_in_dim(dense, offset, rhs_parent.shape[0], 0) + rhs_parent.astype(
        jnp.float32
    )
    return lax.dynamic_update_slice_in_dim(dense, own_rows, offset, 0)


def per_device(rhs_leaf, rhs_parent, inv_leaf, panel, row_map, inv_parent):
    leaf_part = jnp.dot(inv_leaf[0], rhs_leaf[0], preferred_element_type=jnp.float32)
    forward = lax.psum(leaf_part, "col").astype(jnp.bfloat16)
    update = jnp.dot(panel[0], forward, preferred_element_type=jnp.float32)
    dense = dense_updates(update, row_map, rhs_parent)
    leaf_block = lax.psum_scatter(dense, "leaf", scatter_dimension=0, tiled=True)
    reduced = lax.psum(leaf_block, ("row", "col")).astype(jnp.bfloat16)
    parent_part = jnp.dot(inv_parent, reduced, preferred_element_type=jnp.float32)
    fwd_parent = lax.psum(parent_part, "leaf").astype(jnp.bfloat16)
    back_part = lax.dot_general(
        inv_parent, fwd_parent, (((0,), (0,)), ((), ())), preferred_element_type=jnp.float32
    )
    sol_parent = lax.psum_scatter(
        back_part, ("row", "col"), scatter_dimension=0, tiled=True
    ).astype(jnp.bfloat16)
    whole_parent = lax.all_gather(sol_parent, ("leaf", "row", "col"), axis=0, tiled=True)
    picked = jnp.take(whole_parent, row_map[0], axis=0)
    coupling_part = lax.dot_general(
        panel[0], picked, (((0,), (0,)), ((), ())), preferred_element_type=jnp.float32
    )
    coupling = lax.psum(coupling_part, "col")
    corrected = (forward.astype(jnp.float32) - coupling).astype(jnp.bfloat16)
    final_part = lax.dot_general(
        inv_leaf[0], corrected, (((0,), (0,)), ((), ())), preferred_element_type=jnp.float32
    )
    sol_leaf = lax.psum(final_part, "row").astype(jnp.bfloat16)
    return (sol_leaf[None], sol_parent)


def solution(mesh):
    in_specs = (
        P("leaf", "col", None),
        P(("leaf", "row", "col"), None),
        P("leaf", "row", "col"),
        P("leaf", "col", "row"),
        P("leaf", "col"),
        P(("row", "col"), "leaf"),
    )
    out_specs = (P("leaf", "col", None), P(("leaf", "row", "col"), None))
    return jax.shard_map(
        per_device, mesh=mesh, in_specs=in_specs, out_specs=out_specs, check_vma=False
    )
```

profile of v0, /device:TPU:0, one launch (start us, length us, event | category | flops | bytes accessed | tf_op | source)
XLA Modules:
  0.0 728.7 jit_solution(5863380692495050478)
XLA Ops:
  7.2 0.0 copy-start
  7.2 0.0 reduce-scatter.3.cloned.1.call-start
  7.2 1.1 copy-done
  8.3 8.0 %fusion.2 = f32[3072,256]{1,0:T(8,128)} fusion(bf16[1,3072,1536]{2,1,0:T(8,128)(2,1)} %param.8, bf16[1,1536,256]{2,1,0:T(8,128)(2,1)S(1)} %copy-done), kind=kOutput, calls=%fused_computation.4 | convolution fusion | flops 2415919104 | bytes 13369344 | tf_op jit(solution)/shard_map/dot_general | solution.py:19
  16.3 56.8 %all-reduce.7 = bf16[3072,256]{1,0:T(8,128)(2,1)S(1)} all-reduce(f32[3072,256]{1,0:T(8,128)} %fusion.2), channel_id=1, replica_groups=mesh['leaf'=4,'row'=4,'col'=8] {'col'}, use_global_device_ids=true, to_apply=%region_0.0 | all-reduce | flops 786432 | bytes 4718592 | tf_op jit(solution)/shard_map/psum | solution.py:20
  73.1 0.0 copy-start.4
  73.1 3.8 fusion.21
  76.9 0.3 copy.12
  77.1 0.0 copy-done.4
  77.2 0.0 copy-start.3
  77.2 12.3 %scatter_custom_fusion = f32[16384,256]{1,0:T(8,128)} fusion(s32[768]{0:T(1024)S(1)} %fusion.34, f32[768,256]{1,0:T(8,128)S(1)} %copy.12, f32[]{:T(128)} %constant.14.clone.1), kind=kCustom, calls=%fused_computation.6 | custom fusion | flops 196608 | bytes 16777220 | tf_op jit(solution)/shard_map/scatter-add | solution.py:10
  89.5 0.0 copy-done.3
  89.5 1.6 add_dynamic-update-slice_fusion
  91.0 0.0 reduce-scatter.3.cloned.1.call-update
  91.0 0.0 reduce-scatter.5.cloned.1.call-start
  91.1 148.2 %reduce-scatter.3.cloned.1.call-done = f32[4096,256]{1,0:T(8,128)} async-done(((f32[16384,256]{1,0:T(8,128)}), f32[4096,256]{1,0:T(8,128)}) %reduce-scatter.3.cloned.1.call-update) | async-done | bytes 4194320 | tf_op jit(solution)/shard_map/reduce_scatter | solution.py:23
  239.3 153.3 %all-reduce.8 = bf16[4096,256]{1,0:T(8,128)(2,1)} all-reduce(f32[4096,256]{1,0:T(8,128)} %reduce-scatter.3.cloned.1.call-done), channel_id=1, replica_groups=mesh['leaf'=4,'row'=4,'col'=8] {'row','col'}, use_global_device_ids=true, to_apply=%region_3.0 | all-reduce | flops 1048576 | bytes 6291456 | tf_op jit(solution)/shard_map/psum | solution.py:24
  392.6 4.1 fusion.24
  396.8 20.8 %all-reduce.9 = bf16[512,256]{0,1:T(8,128)(2,1)S(1)} all-reduce(f32[512,256]{0,1:T(8,128)S(1)} %fusion.24), channel_id=1, replica_groups=mesh['leaf'=4,'row'=4,'col'=8] {'leaf'}, use_global_device_ids=true, to_apply=%region_4.0 | all-reduce | flops 131072 | bytes 786432 | tf_op jit(solution)/shard_map/psum | solution.py:26
  417.6 5.4 convolution_bitcast_fusion
  423.0 0.0 reduce-scatter.5.cloned.1.call-update
  423.0 0.0 all-gather.2.cloned.1.call-start
  423.1 76.9 %reduce-scatter.5.cloned.1.call-done = f32[128,256]{0,1:T(8,128)} async-done(((f32[4096,256]{0,1:T(8,128)}), f32[128,256]{0,1:T(8,128)}) %reduce-scatter.5.cloned.1.call-update) | async-done | bytes 131088 | tf_op jit(solution)/shard_map/reduce_scatter | solution.py:30
  500.0 1.5 convert_element_type.29
  501.5 0.0 all-gather.2.cloned.1.call-update
  501.5 0.0 all-reduce.6.cloned.1.call-start
  501.6 80.3 %all-gather.2.cloned.1.call-done = bf16[16384,256]{0,1:T(8,128)(2,1)} async-done(((bf16[128,256]{0,1:T(8,128)(2,1)}), bf16[16384,256]{0,1:T(8,128)(2,1)}) %all-gather.2.cloned.1.call-update) | async-done | bytes 8388624 | tf_op jit(solution)/shard_map/all_gather | solution.py:33
  581.9 11.9 %copy.13 = bf16[16384,256]{1,0:T(8,128)(2,1)} copy(bf16[16384,256]{0,1:T(8,128)(2,1)} %all-gather.2.cloned.1.call-done) | data formatting | bytes 16777216 | tf_op jit(solution)/shard_map/all_gather | solution.py:33
  593.8 6.6 gather_fusion
  600.3 0.0 copy-start.2
  600.3 6.1 fusion.10
  606.5 0.0 all-reduce.6.cloned.1.call-update
  606.5 0.0 copy-done.2
  606.5 0.7 copy.15
  607.3 68.0 %all-reduce.6.cloned.1.call-done = f32[3072,256]{1,0:T(8,128)} async-done(((f32[3072,256]{1,0:T(8,128)}), f32[3072,256]{1,0:T(8,128)}) %all-reduce.6.cloned.1.call-update) | async-done | bytes 3145744 | tf_op jit(solution)/shard_map/psum | solution.py:38
  675.3 0.0 copy-start.1
  675.3 8.5 %fusion.13 = f32[1536,256]{0,1:T(8,128)} fusion(bf16[1,3072,1536]{2,1,0:T(8,128)(2,1)} %param.8, f32[3072,256]{1,0:T(8,128)} %all-reduce.6.cloned.1.call-done, bf16[3072,256]{1,0:T(8,128)(2,1)S(1)} %all-reduce.7), kind=kOutput, calls=%fused_computation.15 | convolution fusion | flops 2418278400 | bytes 15728640 | tf_op jit(solution)/shard_map/dot_general | solution.py:40
  683.7 37.3 %all-reduce.10 = bf16[1536,256]{0,1:T(8,128)(2,1)S(1)} all-reduce(f32[1536,256]{0,1:T(8,128)} %fusion.13), channel_id=1, replica_groups=mesh['leaf'=4,'row'=4,'col'=8] {'row'}, use_global_device_ids=true, to_apply=%region_7.8 | all-reduce | flops 393216 | bytes 2359296 | tf_op jit(solution)/shard_map/psum | solution.py:43
  721.0 1.2 copy.14
  722.2 0.0 copy-done.1
  (4 shorter events, 0.0 us)
Async XLA Ops:
  7.2 1.1 copy-start
  7.2 232.2 %reduce-scatter.3.cloned.1.call-start = ((), (), s32[]{:S(2)}) async-start(), calls=%async_computation.2 | async-start | bytes 20971520 | tf_op jit(solution)/shard_map/reduce_scatter | solution.py:23
  73.1 4.1 copy-start.4
  77.2 12.3 %copy-start.3 = (bf16[128,256]{1,0:T(8,128)(2,1)S(1)}, bf16[128,256]{1,0:T(8,128)(2,1)}, u32[]{:S(2)}) copy-start(bf16[128,256]{1,0:T(8,128)(2,1)} %param.7) | copy-start | bytes 196612
  91.0 408.9 %reduce-scatter.5.cloned.1.call-start = ((), (), s32[]{:S(2)}) async-start(), calls=%async_computation.3 | async-start | bytes 4325376 | tf_op jit(solution)/shard_map/reduce_scatter | solution.py:30
  423.0 158.9 %all-gather.2.cloned.1.call-start = ((), (), s32[]{:S(2)}) async-start(), calls=%async_computation.4 | async-start | bytes 8454144 | tf_op jit(solution)/shard_map/all_gather | solution.py:33
  501.5 173.7 %all-reduce.6.cloned.1.call-start = ((), (), s32[]{:S(2)}) async-start(), calls=%async_computation.5 | async-start | bytes 6291456 | tf_op jit(solution)/shard_map/psum | solution.py:38
  600.3 6.2 copy-start.2
  675.3 46.9 %copy-start.1 = (bf16[1,1536,256]{2,1,0:T(8,128)(2,1)S(1)}, bf16[1,1536,256]{2,1,0:T(8,128)(2,1)}, u32[]{:S(2)}) copy-start(bf16[1,1536,256]{2,1,0:T(8,128)(2,1)} %param.6) | copy-start | bytes 2359300
Sparse Core Ops, SparseCore 0:
  91.2 148.1 reduce-scatter.2
  423.1 76.8 reduce-scatter.4
  503.4 78.4 all-gather.1
  606.6 68.5 all-reduce.5
where the time goes:
time: 729 us
  waiting for transfers between devices  374 us (51%)
  blocking collectives  268 us (37%)
  matrix products  35.8 us (5%)
  local copies, waits for them, and re-layouts  21.7 us (3%)
  other arithmetic  15.4 us (2%)
  between operations  13.9 us (2%)
    psum x1, blocking collectives, per_device(): reduced = lax.psum(leaf_block, ('row', 'col')).astype(jnp.bfloat16)  153 us
    reduce_scatter x1, waiting for transfers between devices, per_device(): lax.psum_scatter(dense, 'leaf', scatter_dimension=0, tiled=True)  148 us
    all_gather x1, waiting for transfers between devices, per_device(): lax.all_gather(sol_parent, ('leaf', 'row', 'col'), axis=0, tiled=True)  80.3 us
    reduce_scatter x1, waiting for transfers between devices, per_device(): lax.psum_scatter(back_part, ('row', 'col'), scatter_dimension=0, tiled=True)  76.9 us
    psum x1, waiting for transfers between devices, per_device(): coupling = lax.psum(coupling_part, 'col')  68 us
    psum x1, blocking collectives, per_device(): forward = lax.psum(leaf_part, 'col').astype(jnp.bfloat16)  56.8 us
    psum x1, blocking collectives, per_device(): sol_leaf = lax.psum(final_part, 'row').astype(jnp.bfloat16)  37.3 us
    psum x1, blocking collectives, per_device(): fwd_parent = lax.psum(parent_part, 'leaf').astype(jnp.bfloat16)  20.8 us
  transfers between devices with their start and end apart: 4, of which 4 were waited for; matrix products, arithmetic and copies ran while one was open for 0% of the time, Pallas kernels for 0%

commit v1 on v0

--- a/solution.py
+++ b/solution.py
@@ -35,7 +35,9 @@
     coupling_part = lax.dot_general(
         panel[0], picked, (((0,), (0,)), ((), ())), preferred_element_type=jnp.float32
     )
-    coupling = lax.psum(coupling_part, "col")
+    coupling = coupling_part
+    for hop in (1, 2, 4):
+        coupling = coupling + lax.ppermute(coupling, "col", [(dev, dev ^ hop) for dev in range(8)])
     corrected = (forward.astype(jnp.float32) - coupling).astype(jnp.bfloat16)
     final_part = lax.dot_general(
         inv_leaf[0], corrected, (((0,), (0,)), ((), ())), preferred_element_type=jnp.float32

time: 729 us -> 807 us (1.11)
  waiting for transfers between devices: 374 us -> 449 us
    ppermute x0 -> x3, waiting for transfers between devices: none -> 143 us  [per_device(): lax.ppermute(coupling, 'col', [(dev, dev ^ hop) for dev in range(8)])]
    psum x1 -> x0, waiting for transfers between devices: 68 us -> none  [per_device(): coupling = lax.psum(coupling_part, 'col')]
  transfers between devices with their start and end apart: 4 -> 6, of which waited for: 4 -> 6; matrix products, arithmetic and copies ran while one was open for 0% -> 0% of each run, Pallas kernels for 0% -> 0%
where the time goes in v1:
time: 807 us; the launch traced here: 806 us
  waiting for transfers between devices  449 us (56%)
  blocking collectives  267 us (33%)
  matrix products  33.9 us (4%)
  local copies, waits for them, and re-layouts  21.7 us (3%)
  other arithmetic  17.9 us (2%)
  between operations  13.9 us (2%)
    psum x1, blocking collectives, per_device(): reduced = lax.psum(leaf_block, ('row', 'col')).astype(jnp.bfloat16)  153 us
    reduce_scatter x1, waiting for transfers between devices, per_device(): lax.psum_scatter(dense, 'leaf', scatter_dimension=0, tiled=True)  148 us
    ppermute x3, waiting for transfers between devices, per_device(): lax.ppermute(coupling, 'col', [(dev, dev ^ hop) for dev in range(8)])  143 us
    all_gather x1, waiting for transfers between devices, per_device(): lax.all_gather(sol_parent, ('leaf', 'row', 'col'), axis=0, tiled=True)  80.3 us
    reduce_scatter x1, waiting for transfers between devices, per_device(): lax.psum_scatter(back_part, ('row', 'col'), scatter_dimension=0, tiled=True)  76.9 us
    psum x1, blocking collectives, per_device(): forward = lax.psum(leaf_part, 'col').astype(jnp.bfloat16)  56.8 us
    psum x1, blocking collectives, per_device(): sol_leaf = lax.psum(final_part, 'row').astype(jnp.bfloat16)  36.3 us
    psum x1, blocking collectives, per_device(): fwd_parent = lax.psum(parent_part, 'leaf').astype(jnp.bfloat16)  20.8 us
  transfers between devices with their start and end apart: 6, of which 6 were waited for; matrix products, arithmetic and copies ran while one was open for 0% of the time, Pallas kernels for 0%

profile of v1, /device:TPU:0, one launch (start us, length us, event | category | flops | bytes accessed | tf_op | source)
XLA Modules:
  0.0 806.5 jit_solution(17343921755438290807)
XLA Ops:
  7.2 0.0 copy-start
  7.2 0.0 reduce-scatter.3.cloned.1.call-start
  7.2 1.1 copy-done
  8.3 8.0 fusion.2
  16.3 56.8 %all-reduce.4 = bf16[3072,256]{1,0:T(8,128)(2,1)S(1)} all-reduce(f32[3072,256]{1,0:T(8,128)} %fusion.2), channel_id=1, replica_groups=mesh['leaf'=4,'row'=4,'col'=8] {'col'}, use_global_device_ids=true, to_apply=%region_0.0 | all-reduce | flops 786432 | bytes 4718592 | tf_op jit(solution)/shard_map/psum | solution.py:20
  73.1 0.0 copy-start.2
  73.1 0.0 copy-start.5
  73.1 4.3 fusion.21
  77.4 0.0 copy-done.2
  77.5 0.3 copy.13
  77.7 0.0 copy-done.5
  77.8 0.0 copy-start.4
  77.8 12.3 %scatter_custom_fusion = f32[16384,256]{1,0:T(8,128)} fusion(s32[768]{0:T(1024)S(1)} %fusion.34, f32[768,256]{1,0:T(8,128)S(1)} %copy.13, f32[]{:T(128)} %constant.14.clone.1), kind=kCustom, calls=%fused_computation.6 | custom fusion | flops 196608 | bytes 16777220 | tf_op jit(solution)/shard_map/scatter-add | solution.py:10
  90.0 0.0 copy-done.4
  90.0 1.6 add_dynamic-update-slice_fusion
  91.6 0.0 reduce-scatter.3.cloned.1.call-update
  91.6 0.0 reduce-scatter.5.cloned.1.call-start
  91.7 148.2 %reduce-scatter.3.cloned.1.call-done = f32[4096,256]{1,0:T(8,128)} async-done(((f32[16384,256]{1,0:T(8,128)}), f32[4096,256]{1,0:T(8,128)}) %reduce-scatter.3.cloned.1.call-update) | async-done | bytes 4194320 | tf_op jit(solution)/shard_map/reduce_scatter | solution.py:23
  239.9 152.9 %all-reduce.5 = bf16[4096,256]{1,0:T(8,128)(2,1)S(1)} all-reduce(f32[4096,256]{1,0:T(8,128)} %reduce-scatter.3.cloned.1.call-done), channel_id=1, replica_groups=mesh['leaf'=4,'row'=4,'col'=8] {'row','col'}, use_global_device_ids=true, to_apply=%region_3.0 | all-reduce | flops 1048576 | bytes 6291456 | tf_op jit(solution)/shard_map/psum | solution.py:24
  392.8 3.5 fusion.24
  396.3 20.8 %all-reduce.6 = bf16[512,256]{0,1:T(8,128)(2,1)S(1)} all-reduce(f32[512,256]{0,1:T(8,128)S(1)} %fusion.24), channel_id=1, replica_groups=mesh['leaf'=4,'row'=4,'col'=8] {'leaf'}, use_global_device_ids=true, to_apply=%region_4.0 | all-reduce | flops 131072 | bytes 786432 | tf_op jit(solution)/shard_map/psum | solution.py:26
  417.1 5.4 convolution_bitcast_fusion
  422.5 0.0 reduce-scatter.5.cloned.1.call-update
  422.5 0.0 all-gather.2.cloned.1.call-start
  422.6 76.9 %reduce-scatter.5.cloned.1.call-done = f32[128,256]{0,1:T(8,128)} async-done(((f32[4096,256]{0,1:T(8,128)}), f32[128,256]{0,1:T(8,128)}) %reduce-scatter.5.cloned.1.call-update) | async-done | bytes 131088 | tf_op jit(solution)/shard_map/reduce_scatter | solution.py:30
  499.5 1.5 convert_element_type.29
  501.0 0.0 all-gather.2.cloned.1.call-update
  501.1 80.3 %all-gather.2.cloned.1.call-done = bf16[16384,256]{0,1:T(8,128)(2,1)} async-done(((bf16[128,256]{0,1:T(8,128)(2,1)}), bf16[16384,256]{0,1:T(8,128)(2,1)}) %all-gather.2.cloned.1.call-update) | async-done | bytes 8388624 | tf_op jit(solution)/shard_map/all_gather | solution.py:33
  581.4 11.9 %copy.14 = bf16[16384,256]{1,0:T(8,128)(2,1)} copy(bf16[16384,256]{0,1:T(8,128)(2,1)} %all-gather.2.cloned.1.call-done) | data formatting | bytes 16777216 | tf_op jit(solution)/shard_map/all_gather | solution.py:33
  593.3 6.6 gather_fusion
  599.8 4.4 fusion.10
  604.3 0.3 collective-permute-start
  604.6 5.4 collective-permute-done
  610.0 0.4 add.67
  610.4 0.0 copy-start.3
  610.4 1.3 collective-permute-start.1
  611.7 69.1 %collective-permute-done.1 = f32[3072,256]{1,0:T(8,128)S(1)} collective-permute-done((f32[3072,256]{1,0:T(8,128)S(1)}, f32[3072,256]{1,0:T(8,128)S(1)}, u32[]{:S(2)}, u32[]{:S(2)}) %collective-permute-start.1) | collective-permute-done | bytes 3145760 | tf_op jit(solution)/shard_map/ppermute | solution.py:40
  680.8 2.1 add.68
  682.8 1.8 collective-permute-start.2
  684.6 0.0 copy-done.3
  684.6 0.7 copy.17
  685.3 68.8 %collective-permute-done.2 = f32[3072,256]{1,0:T(8,128)} collective-permute-done((f32[3072,256]{1,0:T(8,128)}, f32[3072,256]{1,0:T(8,128)}, u32[]{:S(2)}, u32[]{:S(2)}) %collective-permute-start.2) | collective-permute-done | bytes 3145760 | tf_op jit(solution)/shard_map/ppermute | solution.py:40
  754.1 0.0 copy-start.1
  754.1 8.4 %fusion.13 = f32[1536,256]{0,1:T(8,128)S(1)} fusion(bf16[1,3072,1536]{2,1,0:T(8,128)(2,1)} %param.8, f32[3072,256]{1,0:T(8,128)} %add.68, f32[3072,256]{1,0:T(8,128)} %collective-permute-done.2, bf16[3072,256]{1,0:T(8,128)(2,1)} %copy-done.2), kind=kOutput, calls=%fused_computation.15 | convolution fusion | flops 2419064832 | bytes 18874368 | tf_op jit(solution)/shard_map/dot_general | solution.py:42
  762.5 36.3 %all-reduce.7 = bf16[1536,256]{0,1:T(8,128)(2,1)S(1)} all-reduce(f32[1536,256]{0,1:T(8,128)S(1)} %fusion.13), channel_id=1, replica_groups=mesh['leaf'=4,'row'=4,'col'=8] {'row'}, use_global_device_ids=true, to_apply=%region_6.7 | all-reduce | flops 393216 | bytes 2359296 | tf_op jit(solution)/shard_map/psum | solution.py:45
  798.8 1.2 copy.16
  799.9 0.0 copy-done.1
  (4 shorter events, 0.0 us)
Async XLA Ops:
  7.2 1.1 copy-start
  7.2 232.7 %reduce-scatter.3.cloned.1.call-start = ((), (), s32[]{:S(2)}) async-start(), calls=%async_computation.2 | async-start | bytes 20971520 | tf_op jit(solution)/shard_map/reduce_scatter | solution.py:23
  73.1 4.4 copy-start.2
  73.1 4.6 copy-start.5
  77.8 12.3 %copy-start.4 = (bf16[128,256]{1,0:T(8,128)(2,1)S(1)}, bf16[128,256]{1,0:T(8,128)(2,1)}, u32[]{:S(2)}) copy-start(bf16[128,256]{1,0:T(8,128)(2,1)} %param.7) | copy-start | bytes 196612
  91.6 407.9 %reduce-scatter.5.cloned.1.call-start = ((), (), s32[]{:S(2)}) async-start(), calls=%async_computation.3 | async-start | bytes 4325376 | tf_op jit(solution)/shard_map/reduce_scatter | solution.py:30
  422.5 158.9 %all-gather.2.cloned.1.call-start = ((), (), s32[]{:S(2)}) async-start(), calls=%async_computation.4 | async-start | bytes 8454144 | tf_op jit(solution)/shard_map/all_gather | solution.py:33
  604.3 5.7 collective-permute-start
  610.4 74.2 %copy-start.3 = (bf16[128,256]{0,1:T(8,128)(2,1)S(1)}, bf16[128,256]{0,1:T(8,128)(2,1)}, u32[]{:S(2)}) copy-start(bf16[128,256]{0,1:T(8,128)(2,1)} %convert_element_type.29) | copy-start | bytes 196612
  610.4 70.3 %collective-permute-start.1 = (f32[3072,256]{1,0:T(8,128)S(1)}, f32[3072,256]{1,0:T(8,128)S(1)}, u32[]{:S(2)}, u32[]{:S(2)}) collective-permute-start(f32[3072,256]{1,0:T(8,128)S(1)} %add.67), channel_id=1, source_target_pairs={{0,2},{1,3},{2,0},{3,1},{4,6},{5,7},{6,4},{7,5},{8,10},{9,11},{10,... | collective-permute-start | bytes 9437192 | tf_op jit(solution)/shard_map/ppermute | solution.py:40
  682.8 71.3 %collective-permute-start.2 = (f32[3072,256]{1,0:T(8,128)}, f32[3072,256]{1,0:T(8,128)}, u32[]{:S(2)}, u32[]{:S(2)}) collective-permute-start(f32[3072,256]{1,0:T(8,128)} %add.68), channel_id=1, source_target_pairs={{0,4},{1,5},{2,6},{3,7},{4,0},{5,1},{6,2},{7,3},{8,12},{9,13},{10,... | collective-permute-start | bytes 9437192 | tf_op jit(solution)/shard_map/ppermute | solution.py:40
  754.1 45.8 %copy-start.1 = (bf16[1,1536,256]{2,1,0:T(8,128)(2,1)S(1)}, bf16[1,1536,256]{2,1,0:T(8,128)(2,1)}, u32[]{:S(2)}) copy-start(bf16[1,1536,256]{2,1,0:T(8,128)(2,1)} %param.6) | copy-start | bytes 2359300
Sparse Core Ops, SparseCore 0:
  91.7 148.1 reduce-scatter.2
  422.6 76.8 reduce-scatter.4
  502.9 78.4 all-gather.1
